TPU v7x, 32 devices: a whole 2x2x4 slice. The times are simulated.
32 devices in a mesh: dp: 16 (over z, y, x), grp: 2 (over core).
Axes of the slice: x: 2, y: 2, z: 4, core: 2. Of those that a mesh axis runs over, the one named last changes fastest.
Arguments:
- query_features: bfloat16 [32768, 512], P(('dp', 'grp')), may hold values from -256 to 256
- query_weights: bfloat16 [32768], P(('dp', 'grp')), may hold values from 0.5 to 13.5, as said below
- positive_index: int32 [32768], P(('dp', 'grp')), may hold values from 0 to 511
- item_features: bfloat16 [512, 512], P(('dp', 'grp')), may hold values from -6 to 6
- item_ids: int32 [512], P(('dp', 'grp')), may hold values from 0 to 255
- item_logq: bfloat16 [512], P(('dp', 'grp')), may hold values from -14 to -11
- query_w_in: bfloat16 [512, 1024], replicated, may hold values from -0.25 to 0.25
- query_w_out: bfloat16 [1024, 256], replicated, may hold values from -0.1875 to 0.1875
- item_w_in: bfloat16 [512, 1024], replicated, may hold values from -0.25 to 0.25
- item_w_out: bfloat16 [1024, 256], replicated, may hold values from -0.1875 to 0.1875
Outputs:
- grad_query_w_in: float32 [512, 1024], replicated
- grad_query_w_out: float32 [1024, 256], replicated
- grad_item_w_in: float32 [512, 1024], replicated
- grad_item_w_out: float32 [1024, 256], replicated
Inputs may be any that keep to these rules, and one draw needn't show every extreme that they name: `query_weights`: positive weights. `item_ids`: an id may occur several times in the sample set.
All inputs are finite; a program needn't handle non-finite values.
Results may differ from a plain program's by a relative error of at most 0.013.
Values may be sent and summed in bfloat16 or wider, within the bound.
A program may use at most 128 MiB of HBM per device.

v0:
```python
import jax
import jax.numpy as jnp
from jax import lax
from jax.sharding import PartitionSpec as P

score_scale = 0.25
loss_scale = 1024.0


def silu_slope(values):
    gate = jax.nn.sigmoid(values)
    return gate * (1.0 + values * (1.0 - gate))


def tower(features, weight_in, weight_out):
    pre_act = jnp.dot(features, weight_in, preferred_element_type=jnp.float32)
    hidden = jax.nn.silu(pre_act).astype(jnp.bfloat16)
    embedding = jnp.dot(hidden, weight_out, preferred_element_type=jnp.float32).astype(jnp.bfloat16)
    return (pre_act, hidden, embedding)


def tower_back(features, pre_act, hidden, weight_out, embed_grad):
    grad_out = jnp.dot(hidden.T, embed_grad, preferred_element_type=jnp.float32)
    hidden_grad = jnp.dot(embed_grad, weight_out.T, preferred_element_type=jnp.float32)
    pre_grad = (hidden_grad * silu_slope(pre_act)).astype(jnp.bfloat16)
    grad_in = jnp.dot(features.T, pre_grad, preferred_element_type=jnp.float32)
    return (grad_in, grad_out)


def item_scores(query_rows, items, item_bias, item_codes, columns, positives, pos_codes):
    raw_scores = lax.dot_general(
        query_rows, items, (((1,), (1,)), ((), ())), preferred_element_type=jnp.float32
    )
    scores = score_scale * raw_scores - item_bias.astype(jnp.float32)[None, :]
    masked_hits = (item_codes[None, :] == pos_codes[:, None]) & (
        columns[None, :] != positives[:, None]
    )
    return jnp.where(masked_hits, -jnp.inf, scores)


def partial_stats(scores):
    row_max = jnp.maximum(jnp.max(scores, axis=1), -1e30)
    row_sum = jnp.sum(jnp.exp(scores - row_max[:, None]), axis=1)
    return (row_max, row_sum)


def finish(scores, row_max, row_sum, columns, positives, weights):
    probability = jnp.exp(scores - row_max[:, None]) / row_sum[:, None]
    target = (columns[None, :] == positives[:, None]).astype(jnp.float32)
    return (weights.astype(jnp.float32)[:, None] * (probability - target)).astype(jnp.bfloat16)


def positive_codes(every_code, positives):
    slots = jnp.arange(every_code.shape[0], dtype=jnp.int32)
    return jnp.sum(jnp.where(positives[:, None] == slots[None, :], every_code[None, :], 0), axis=1)


def on_device(
    query_features,
    query_weights,
    positive_index,
    item_features,
    item_ids,
    item_logq,
    query_w_in,
    query_w_out,
    item_w_in,
    item_w_out,
):
    weight_part = jnp.sum(query_weights.astype(jnp.float32))
    weight_total = lax.psum(weight_part, ("dp", "grp"))
    query_pre, query_hidden, query_embed = tower(query_features, query_w_in, query_w_out)
    item_pre, item_hidden, item_embed = tower(item_features, item_w_in, item_w_out)
    items_all, bias_all, codes_all = (
        lax.all_gather(item_embed, ("dp", "grp"), axis=0, tiled=True),
        lax.all_gather(item_logq, ("dp", "grp"), axis=0, tiled=True),
        lax.all_gather(item_ids, ("dp", "grp"), axis=0, tiled=True),
    )
    columns = jnp.arange(items_all.shape[0], dtype=jnp.int32)
    pos_codes = positive_codes(codes_all, positive_index)
    scores = item_scores(
        query_embed, items_all, bias_all, codes_all, columns, positive_index, pos_codes
    )
    row_max, row_sum = partial_stats(scores)
    dlogit = finish(scores, row_max, row_sum, columns, positive_index, query_weights)
    query_grad = (
        score_scale * jnp.dot(dlogit, items_all, preferred_element_type=jnp.float32)
    ).astype(jnp.bfloat16)
    item_grad = lax.psum_scatter(
        score_scale
        * lax.dot_general(
            dlogit, query_embed, (((0,), (0,)), ((), ())), preferred_element_type=jnp.float32
        ),
        ("dp", "grp"),
        scatter_dimension=0,
        tiled=True,
    ).astype(jnp.bfloat16)
    query_in_part, query_out_part = tower_back(
        query_features, query_pre, query_hidden, query_w_out, query_grad
    )
    item_in_part, item_out_part = tower_back(
        item_features, item_pre, item_hidden, item_w_out, item_grad
    )
    query_in_sum, query_out_sum, item_in_sum, item_out_sum = lax.psum(
        (query_in_part, query_out_part, item_in_part, item_out_part), ("dp", "grp")
    )
    factor = loss_scale / weight_total
    return (
        query_in_sum * factor,
        query_out_sum * factor,
        item_in_sum * factor,
        item_out_sum * factor,
    )


def solution(mesh):
    in_specs = (
        P(("dp", "grp"), None),
        P(("dp", "grp")),
        P(("dp", "grp")),
        P(("dp", "grp"), None),
        P(("dp", "grp")),
        P(("dp", "grp")),
        P(),
        P(),
        P(),
        P(),
    )
    out_specs = (P(), P(), P(), P())
    return jax.shard_map(
        on_device, mesh=mesh, in_specs=in_specs, out_specs=out_specs, check_vma=False
    )
```

profile of v0, /device:TPU:0, one launch (start us, length us, event | category | flops | bytes accessed | tf_op | source)
XLA Modules:
  0.0 457.4 jit_solution(10545431475410207212)
XLA Ops:
  7.2 0.0 copy-start
  7.2 0.0 reduce-scatter.2.cloned.1.call-start
  7.2 1.6 fusion.16
  8.8 1.2 convolution_convert_fusion.1
  10.0 43.9 %all_gather.10 = bf16[512,256]{1,0:T(8,128)(2,1)S(1)} all-gather(bf16[16,256]{1,0:T(8,128)(2,1)S(1)} %convolution_convert_fusion.1), channel_id=1, replica_groups=mesh['dp'=16,'grp'=2] {'dp','grp'}, dimensions={0}, use_global_device_ids=true | all-gather | bytes 270336 | tf_op jit(solution)/shard_map/all_gather | solution.py:75
  54.0 0.8 dynamic-update-slice
  54.8 36.8 %all-reduce = s32[512]{0:T(512)S(1)} all-reduce(s32[512]{0:T(512)S(1)} %dynamic-update-slice), channel_id=1, replica_groups=mesh['dp'=16,'grp'=2] {'dp','grp'}, use_global_device_ids=true, to_apply=%add | all-reduce | flops 512 | bytes 4096
  91.6 0.8 dynamic-update-slice.1
  92.5 41.1 %all-reduce.1 = bf16[512]{0:T(512)(128)(2,1)S(1)} all-reduce(bf16[512]{0:T(512)(128)(2,1)S(1)} %dynamic-update-slice.1), channel_id=1, replica_groups=mesh['dp'=16,'grp'=2] {'dp','grp'}, use_global_device_ids=true, to_apply=%add.1 | all-reduce | flops 512 | bytes 2048
  133.6 0.0 copy-done
  133.6 0.0 copy-start.6
  133.6 4.8 %multiply_convert_fusion.1 = (bf16[1024,1024]{1,0:T(8,128)(2,1)S(1)}, f32[1024,1024]{1,0:T(8,128)}) fusion(bf16[1024,512]{1,0:T(8,128)(2,1)S(1)} %copy-done, bf16[512,1024]{1,0:T(8,128)(2,1)} %param.16), kind=kOutput, calls=%fused_computation.1 | convolution fusion | flops 1078984704 | bytes 8388608 | tf_op jit(solution)/shard_map/dot_general | solution.py:16
  138.4 0.0 copy-start.7
  138.4 0.0 copy-done.6
  138.4 0.0 copy-start.4
  138.4 0.7 convolution_convert_fusion
  139.1 0.6 copy-done.7
  139.7 0.0 copy-done.4
  139.7 0.3 select_reduce_fusion
  140.0 0.0 copy-start.5
  140.0 0.8 fusion.15
  140.8 0.0 copy-done.5
  140.8 0.3 fusion.1
  141.2 0.7 multiply_convert_fusion.2
  141.8 1.2 convolution_multiply_fusion.1
  143.1 0.0 reduce-scatter.2.cloned.1.call-update
  143.1 0.0 all-reduce.5.cloned.1.call-start
  143.2 0.0 copy-start.8
  143.2 0.5 fusion.2
  143.7 1.1 copy-done.8
  144.7 1.7 fusion.17
  146.5 0.0 copy-start.1
  146.5 0.0 copy-start.2
  146.5 6.1 %convolution_bitcast_fusion.1 = f32[512,1024]{0,1:T(8,128)} fusion(bf16[1024,512]{1,0:T(8,128)(2,1)S(1)} %copy-done, f32[1024,1024]{1,0:T(8,128)} %get-tuple-element.13, bf16[1024,256]{1,0:T(8,128)(2,1)S(1)} %fusion.2, bf16[1024,256]{1,0:T(8,128)(2,1)S(1)} %copy-done.6), kind=kOutput, calls=%fused_computation.13 | convolution fusion | flops 1620049920 | bytes 8388608 | tf_op jit(solution)/shard_map/dot_general | solution.py:26
  152.5 126.6 %reduce-scatter.2.cloned.1.call-done = f32[16,256]{1,0:T(8,128)} async-done(((f32[512,256]{1,0:T(8,128)}), f32[16,256]{1,0:T(8,128)}) %reduce-scatter.2.cloned.1.call-update) | async-done | bytes 16400 | tf_op jit(solution)/shard_map/reduce_scatter | solution.py:89
  279.2 0.0 copy-done.1
  279.2 0.0 copy-done.2
  279.2 0.0 copy-start.3
  279.2 2.7 convolution_bitcast_fusion
  281.9 0.0 copy-done.3
  281.9 1.3 fusion.9
  283.3 0.0 all-reduce.5.cloned.1.call-update
  283.3 0.6 convert_reduce_fusion
  283.9 38.4 %psum.36 = f32[]{:T(128)} all-reduce(f32[]{:T(128)} %convert_reduce_fusion), channel_id=1, replica_groups=mesh['dp'=16,'grp'=2] {'dp','grp'}, use_global_device_ids=true, to_apply=%region_5.6 | all-reduce | flops 1 | bytes 8 | tf_op jit(solution)/shard_map/psum | solution.py:71
  322.9 115.9 %all-reduce.5.cloned.1.call-done = (f32[512,1024]{0,1:T(8,128)}, f32[1024,256]{1,0:T(8,128)}, f32[512,1024]{0,1:T(8,128)}, f32[1024,256]{1,0:T(8,128)}) async-done(((f32[512,1024]{0,1:T(8,128)}, f32[1024,256]{1,0:T(8,128)}, f32[512,1024]{0,1:T(8,128)}, f32[1024,256]{1,0:T(8,128)}), (f32[512,1024]{0,1:T(8,128)}, f32[1024,256]{1,0:T(8,128)}, f32[512,1024]{0,1:T(8,128)}, ...) | async-done | bytes 6291472 | tf_op jit(solution)/shard_map/psum | solution.py:104
  438.8 4.0 broadcast_multiply_fusion
  442.9 2.9 copy.14
  445.8 1.8 copy.15
  447.6 3.0 broadcast_multiply_fusion.2
  (5 shorter events, 0.0 us)
Async XLA Ops:
  7.2 126.5 %copy-start = (bf16[1024,512]{1,0:T(8,128)(2,1)S(1)}, bf16[1024,512]{1,0:T(8,128)(2,1)}, u32[]{:S(2)}) copy-start(bf16[1024,512]{1,0:T(8,128)(2,1)} %param.10) | copy-start | bytes 3145732
  7.2 272.0 %reduce-scatter.2.cloned.1.call-start = ((), (), s32[]{:S(2)}) async-start(), calls=%async_computation.1 | async-start | bytes 540672 | tf_op jit(solution)/shard_map/reduce_scatter | solution.py:89
  133.6 4.8 %copy-start.6 = (bf16[1024,256]{1,0:T(8,128)(2,1)S(1)}, bf16[1024,256]{1,0:T(8,128)(2,1)}, u32[]{:S(2)}) copy-start(bf16[1024,256]{1,0:T(8,128)(2,1)} %param.17) | copy-start | bytes 1572868
  138.4 1.3 copy-start.7
  138.4 1.3 copy-start.4
  140.0 0.8 copy-start.5
  143.1 295.7 %all-reduce.5.cloned.1.call-start = ((), (), s32[]{:S(2)}) async-start(), calls=%async_computation.2 | async-start | bytes 12582912 | tf_op jit(solution)/shard_map/psum | solution.py:104
  143.2 1.6 copy-start.8
  146.5 132.7 %copy-start.1 = (bf16[1024,256]{1,0:T(8,128)(2,1)S(1)}, bf16[1024,256]{1,0:T(8,128)(2,1)}, u32[]{:S(2)}) copy-start(bf16[1024,256]{1,0:T(8,128)(2,1)} %param.19) | copy-start | bytes 1572868
  146.5 132.7 %copy-start.2 = (bf16[16,512]{1,0:T(8,128)(2,1)S(1)}, bf16[16,512]{1,0:T(8,128)(2,1)}, u32[]{:S(2)}) copy-start(bf16[16,512]{1,0:T(8,128)(2,1)} %param.13) | copy-start | bytes 49156
  279.2 2.8 copy-start.3
Sparse Core Ops, SparseCore 0:
  143.2 135.9 reduce-scatter.1
  285.8 153.0 all-reduce.4
where the time goes:
time: 458 us; the launch traced here: 457 us
  waiting for transfers between devices  243 us (53%)
  blocking collectives  160 us (35%)
  matrix products  22.6 us (5%)
  between operations  14.8 us (3%)
  other arithmetic  8.95 us (2%)
  local copies, waits for them, and re-layouts  8.09 us (2%)
    reduce_scatter x1, waiting for transfers between devices, on_device(): lax.psum_scatter(score_scale * lax.dot_general(dlogit, query_embed, (((0,...  127 us
    psum x1, waiting for transfers between devices, on_device(): lax.psum((query_in_part, query_out_part, item_in_part, item_out_part), ('...  116 us
    unnamed x2, blocking collectives  78 us
    all_gather x1, blocking collectives, on_device(): lax.all_gather(item_embed, ('dp', 'grp'), axis=0, tiled=True)  43.9 us
    psum x1, blocking collectives, on_device(): weight_total = lax.psum(weight_part, ('dp', 'grp'))  38.4 us
  transfers between devices with their start and end apart: 2, of which 2 were waited for; matrix products, arithmetic and copies ran while one was open for 2% of the time, Pallas kernels for 0%

commit v1 on v0

--- a/solution.py
+++ b/solution.py
@@ -5,6 +5,14 @@
 
 score_scale = 0.25
 loss_scale = 1024.0
+
+
+def tiled_gather(shard, axis, dim):
+    size = lax.axis_size(axis)
+    repeats = [size if d == dim else 1 for d in range(shard.ndim)]
+    return lax.all_to_all(
+        jnp.tile(shard, repeats), axis, split_axis=dim, concat_axis=dim, tiled=True
+    )
 
 
 def silu_slope(values):
@@ -72,7 +80,7 @@
     query_pre, query_hidden, query_embed = tower(query_features, query_w_in, query_w_out)
     item_pre, item_hidden, item_embed = tower(item_features, item_w_in, item_w_out)
     items_all, bias_all, codes_all = (
-        lax.all_gather(item_embed, ("dp", "grp"), axis=0, tiled=True),
+        tiled_gather(item_embed, ("dp", "grp"), 0),
         lax.all_gather(item_logq, ("dp", "grp"), axis=0, tiled=True),
         lax.all_gather(item_ids, ("dp", "grp"), axis=0, tiled=True),
     )

time: 458 us -> 425 us (0.928)
  blocking collectives: 160 us -> 119 us
  starting transfers between devices: 0.08 us -> 7.41 us
    all_gather x1 -> x0, blocking collectives: 43.9 us -> none  [on_device(): lax.all_gather(item_embed, ('dp', 'grp'), axis=0, tiled=True)]
    all_to_all x0 -> x1, starting transfers between devices: none -> 7.33 us  [tiled_gather(): lax.all_to_all(jnp.tile(shard, repeats), axis, split_axis=dim, concat_axi...]
  transfers between devices with their start and end apart: 2 -> 3, of which waited for: 2 -> 2; matrix products, arithmetic and copies ran while one was open for 2% -> 4% of each run, Pallas kernels for 0% -> 0%
where the time goes in v1:
time: 425 us
  waiting for transfers between devices  243 us (57%)
  blocking collectives  119 us (28%)
  matrix products  25.3 us (6%)
  between operations  14.8 us (3%)
  other arithmetic  8.95 us (2%)
  starting transfers between devices  7.41 us (2%)
  local copies, waits for them, and re-layouts  5.93 us (1%)
    reduce_scatter x1, waiting for transfers between devices, on_device(): lax.psum_scatter(score_scale * lax.dot_general(dlogit, query_embed, (((0,...  127 us
    psum x1, waiting for transfers between devices, on_device(): lax.psum((query_in_part, query_out_part, item_in_part, item_out_part), ('...  116 us
    unnamed x2, blocking collectives  80.5 us
    psum x1, blocking collectives, on_device(): weight_total = lax.psum(weight_part, ('dp', 'grp'))  38.4 us
    dot_general x2, matrix products, tower_back(): grad_in = jnp.dot(features.T, pre_grad, preferred_element_type=jnp.float32)  8.77 us
  transfers between devices with their start and end apart: 3, of which 2 were waited for; matrix products, arithmetic and copies ran while one was open for 4% of the time, Pallas kernels for 0%

profile of v1, /device:TPU:0, one launch (start us, length us, event | category | flops | bytes accessed | tf_op | source)
XLA Modules:
  0.0 424.7 jit_solution(18428963756166516648)
XLA Ops:
  7.2 0.0 copy-start
  7.2 0.0 copy-start.6
  7.2 1.6 fusion.16
  8.8 1.2 convolution_convert_fusion.1
  10.1 0.7 tile.2
  10.8 7.3 %all-to-all-start = ((bf16[32,16,256]{2,1,0:T(8,128)(2,1)}), bf16[32,16,256]{2,1,0:T(8,128)(2,1)S(1)}, u32[]{:S(2)}, u32[]{:S(2)}) async-start(bf16[32,16,256]{2,1,0:T(8,128)(2,1)} %tile.2), calls=%async_computation | async-start | bytes 524288 | tf_op jit(solution)/shard_map/all_to_all | solution.py:13
  18.1 0.0 copy-start.8
  18.1 0.0 copy-start.5
  18.1 0.0 copy-start.9
  18.2 0.0 copy-start.4
  18.2 0.0 copy-start.7
  18.2 0.0 reduce-scatter.2.cloned.1.call-start
  18.2 0.0 copy-done
  18.2 0.0 copy-done.6
  18.2 4.3 %multiply_convert_fusion.1 = (bf16[1024,1024]{1,0:T(8,128)(2,1)}, f32[1024,1024]{1,0:T(8,128)}) fusion(bf16[1024,512]{1,0:T(8,128)(2,1)S(1)} %copy-done, bf16[512,1024]{1,0:T(8,128)(2,1)S(1)} %copy-done.6), kind=kOutput, calls=%fused_computation.1 | convolution fusion | flops 1078984704 | bytes 8388608 | tf_op jit(solution)/shard_map/dot_general | solution.py:24
  22.5 0.0 copy-done.8
  22.5 0.2 dynamic-update-slice.1
  22.7 40.5 %all-reduce.1 = bf16[512]{0:T(512)(128)(2,1)S(1)} all-reduce(bf16[512]{0:T(512)(128)(2,1)S(1)} %dynamic-update-slice.1), channel_id=1, replica_groups=mesh['dp'=16,'grp'=2] {'dp','grp'}, use_global_device_ids=true, to_apply=%add.1 | all-reduce | flops 512 | bytes 2048
  63.3 0.0 copy-done.5
  63.3 0.0 copy-done.9
  63.3 0.2 dynamic-update-slice
  63.5 40.0 %all-reduce = s32[512]{0:T(512)S(1)} all-reduce(s32[512]{0:T(512)S(1)} %dynamic-update-slice), channel_id=1, replica_groups=mesh['dp'=16,'grp'=2] {'dp','grp'}, use_global_device_ids=true, to_apply=%add | all-reduce | flops 512 | bytes 4096
  103.5 0.0 copy-done.4
  103.5 0.3 select_reduce_fusion
  103.9 0.0 copy-done.7
  103.9 2.3 convolution_convert_fusion
  106.2 0.0 all-to-all-done
  106.2 0.8 fusion.15
  107.0 0.3 fusion.1
  107.3 0.7 multiply_convert_fusion.2
  108.0 1.2 convolution_multiply_fusion.1
  109.2 0.5 fusion.2
  109.7 0.0 reduce-scatter.2.cloned.1.call-update
  109.7 0.0 all-reduce.5.cloned.1.call-start
  109.8 3.3 fusion.17
  113.1 0.0 copy-start.1
  113.1 0.0 copy-start.2
  113.1 6.0 %convolution_bitcast_fusion.1 = f32[512,1024]{0,1:T(8,128)} fusion(bf16[1024,512]{1,0:T(8,128)(2,1)S(1)} %copy-done, f32[1024,1024]{1,0:T(8,128)} %get-tuple-element.13, bf16[1024,256]{1,0:T(8,128)(2,1)S(1)} %fusion.2, bf16[1024,256]{1,0:T(8,128)(2,1)S(1)} %copy-done.7), kind=kOutput, calls=%fused_computation.13 | convolution fusion | flops 1620049920 | bytes 8388608 | tf_op jit(solution)/shard_map/dot_general | solution.py:34
  119.1 127.2 %reduce-scatter.2.cloned.1.call-done = f32[16,256]{1,0:T(8,128)} async-done(((f32[512,256]{1,0:T(8,128)}), f32[16,256]{1,0:T(8,128)}) %reduce-scatter.2.cloned.1.call-update) | async-done | bytes 16400 | tf_op jit(solution)/shard_map/reduce_scatter | solution.py:97
  246.3 0.0 copy-done.1
  246.3 0.0 copy-done.2
  246.3 0.0 copy-start.3
  246.3 2.7 convolution_bitcast_fusion
  249.1 0.0 copy-done.3
  249.1 1.3 fusion.9
  250.4 0.0 all-reduce.5.cloned.1.call-update
  250.4 0.6 convert_reduce_fusion
  251.0 38.4 %psum.36 = f32[]{:T(128)} all-reduce(f32[]{:T(128)} %convert_reduce_fusion), channel_id=1, replica_groups=mesh['dp'=16,'grp'=2] {'dp','grp'}, use_global_device_ids=true, to_apply=%region_5.6 | all-reduce | flops 1 | bytes 8 | tf_op jit(solution)/shard_map/psum | solution.py:79
  290.0 116.1 %all-reduce.5.cloned.1.call-done = (f32[512,1024]{0,1:T(8,128)}, f32[1024,256]{1,0:T(8,128)}, f32[512,1024]{0,1:T(8,128)}, f32[1024,256]{1,0:T(8,128)}) async-done(((f32[512,1024]{0,1:T(8,128)}, f32[1024,256]{1,0:T(8,128)}, f32[512,1024]{0,1:T(8,128)}, f32[1024,256]{1,0:T(8,128)}), (f32[512,1024]{0,1:T(8,128)}, f32[1024,256]{1,0:T(8,128)}, f32[512,1024]{0,1:T(8,128)}, ...) | async-done | bytes 6291472 | tf_op jit(solution)/shard_map/psum | solution.py:112
  406.1 4.0 broadcast_multiply_fusion
  410.1 2.9 copy.14
  413.0 1.8 copy.15
  414.8 3.0 broadcast_multiply_fusion.2
  (5 shorter events, 0.0 us)
Async XLA Ops:
  7.2 11.1 %copy-start = (bf16[1024,512]{1,0:T(8,128)(2,1)S(1)}, bf16[1024,512]{1,0:T(8,128)(2,1)}, u32[]{:S(2)}) copy-start(bf16[1024,512]{1,0:T(8,128)(2,1)} %param.10) | copy-start | bytes 3145732
  7.2 11.1 %copy-start.6 = (bf16[512,1024]{1,0:T(8,128)(2,1)S(1)}, bf16[512,1024]{1,0:T(8,128)(2,1)}, u32[]{:S(2)}) copy-start(bf16[512,1024]{1,0:T(8,128)(2,1)} %param.16) | copy-start | bytes 3145732
  10.8 95.4 %all-to-all-start = ((bf16[32,16,256]{2,1,0:T(8,128)(2,1)}), bf16[32,16,256]{2,1,0:T(8,128)(2,1)S(1)}, u32[]{:S(2)}, u32[]{:S(2)}) async-start(bf16[32,16,256]{2,1,0:T(8,128)(2,1)} %tile.2), calls=%async_computation | async-start | bytes 524288 | tf_op jit(solution)/shard_map/all_to_all | solution.py:13
  18.1 4.4 %copy-start.8 = (bf16[16]{0:T(256)(128)(2,1)S(1)}, bf16[16]{0:T(256)(128)(2,1)}, u32[]{:S(2)}) copy-start(bf16[16]{0:T(256)(128)(2,1)} %param.15) | copy-start | bytes 100
  18.1 45.1 %copy-start.5 = (bf16[1024]{0:T(1024)(128)(2,1)S(1)}, bf16[1024]{0:T(1024)(128)(2,1)}, u32[]{:S(2)}) copy-start(bf16[1024]{0:T(1024)(128)(2,1)} %param.11) | copy-start | bytes 6148
  18.1 45.1 %copy-start.9 = (s32[16]{0:T(128)S(1)}, s32[16]{0:T(128)}, u32[]{:S(2)}) copy-start(s32[16]{0:T(128)} %param.14) | copy-start | bytes 196
  18.2 85.4 %copy-start.4 = (s32[1024]{0:T(1024)S(1)}, s32[1024]{0:T(1024)}, u32[]{:S(2)}) copy-start(s32[1024]{0:T(1024)} %param.12) | copy-start | bytes 12292
  18.2 85.7 %copy-start.7 = (bf16[1024,256]{1,0:T(8,128)(2,1)S(1)}, bf16[1024,256]{1,0:T(8,128)(2,1)}, u32[]{:S(2)}) copy-start(bf16[1024,256]{1,0:T(8,128)(2,1)} %param.17) | copy-start | bytes 1572868
  18.2 228.1 %reduce-scatter.2.cloned.1.call-start = ((), (), s32[]{:S(2)}) async-start(), calls=%async_computation.2 | async-start | bytes 540672 | tf_op jit(solution)/shard_map/reduce_scatter | solution.py:97
  109.7 296.4 %all-reduce.5.cloned.1.call-start = ((), (), s32[]{:S(2)}) async-start(), calls=%async_computation.3 | async-start | bytes 12582912 | tf_op jit(solution)/shard_map/psum | solution.py:112
  113.1 133.2 %copy-start.1 = (bf16[1024,256]{1,0:T(8,128)(2,1)S(1)}, bf16[1024,256]{1,0:T(8,128)(2,1)}, u32[]{:S(2)}) copy-start(bf16[1024,256]{1,0:T(8,128)(2,1)} %param.19) | copy-start | bytes 1572868
  113.1 133.2 %copy-start.2 = (bf16[16,512]{1,0:T(8,128)(2,1)S(1)}, bf16[16,512]{1,0:T(8,128)(2,1)}, u32[]{:S(2)}) copy-start(bf16[16,512]{1,0:T(8,128)(2,1)} %param.13) | copy-start | bytes 49156
  246.3 2.8 copy-start.3
Sparse Core Ops, SparseCore 0:
  109.8 136.4 reduce-scatter.1
  252.9 153.1 all-reduce.4
